TPU v7x, 128 devices: a whole 4x4x4 slice. The times are simulated.
128 devices in a mesh: band: 8 (over y, x_lo), blk: 16 (over z, x_hi, core).
Axes of the slice: x: 4 (x_hi: 2, x_lo: 2; x = x_hi * 2 + x_lo), y: 4, z: 4, core: 2. Of those that a mesh axis runs over, the one named last changes fastest.
Arguments:
- impedance: float32 [8, 2, 6144, 6144], P('band', None, 'blk'), may hold values from -1.3 to 1.3, as said below
- adjoint_source: float32 [8, 2, 32, 6144], P('band', None, None, 'blk'), may hold values from -60 to 60
- currents: float32 [8, 2, 32, 6144], P('band', None, None, 'blk'), may hold values from -6 to 6
- sensitivity: float32 [8, 2, 6144], P('band', None, 'blk'), may hold values from -0.3 to 0.3
- owner: int32 [6144], P('blk'), may hold values from 0 to 4095
Outputs:
- adjoint_field: float32 [8, 2, 32, 6144], P('band', None, None, 'blk')
- design_gradient: float32 [4096], P(('band', 'blk'))
Inputs may be any that keep to these rules, and one draw needn't show every extreme that they name: Read as a complex matrix, each band's impedance matrix is nonsingular.
All inputs are finite; a program needn't handle non-finite values.
Results may differ from a plain program's by a relative error of at most 0.00023.
Values sent between devices are 32-bit elements; how exact they have to be, the bound alone decides.
A program may use at most 192 MiB of HBM per device.

v0:
```python
import jax
import jax.numpy as jnp
from jax import lax
from jax.sharding import PartitionSpec as P

ITERS = 5
DESIGN = 4096


HIGH = lax.Precision.HIGHEST
EPS = 1e-12


def apply_adjoint(panel_real, panel_imag, vector):
    count = vector.shape[1]
    stacked = jnp.concatenate([vector[0], vector[1]], axis=0)
    first = jnp.dot(stacked, panel_real, precision=HIGH, preferred_element_type=jnp.float32)
    second = jnp.dot(stacked, panel_imag, precision=HIGH, preferred_element_type=jnp.float32)
    return jnp.stack([first[:count] + second[count:], first[count:] - second[:count]])


def least_squares(columns, beta):
    count = len(columns)
    cosines = []
    sines = []
    upper = []
    rhs = [beta] + [jnp.zeros_like(beta) for position in range(count)]
    for current in range(count):
        column = list(columns[current])
        for earlier in range(current):
            top = cosines[earlier] * column[earlier] + sines[earlier] * column[earlier + 1]
            column[earlier + 1] = (
                cosines[earlier] * column[earlier + 1] - sines[earlier] * column[earlier]
            )
            column[earlier] = top
        radius = jnp.sqrt(
            column[current] * column[current] + column[current + 1] * column[current + 1]
        )
        cosines.append(column[current] / radius)
        sines.append(column[current + 1] / radius)
        column[current] = radius
        upper.append(column[: current + 1])
        rhs[current + 1] = -sines[current] * rhs[current]
        rhs[current] = cosines[current] * rhs[current]
    weights = [None] * count
    for current in reversed(range(count)):
        total = rhs[current]
        for later in range(current + 1, count):
            total = total - upper[later][current] * weights[later]
        weights[current] = total / upper[current][current]
    return weights


def restarted_solve(source, operator, total, orthogonalize):
    solution = jnp.zeros_like(source)
    beta = jnp.sqrt(total(jnp.sum(source * source, axis=(0, 2))) + EPS)
    basis = [source / beta[None, :, None]]
    columns = []
    for current in range(ITERS):
        image = operator(basis[current])
        image, coeffs, length = orthogonalize(jnp.stack(basis), image)
        columns.append([coeffs[:, earlier] for earlier in range(current + 1)] + [length])
        if current + 1 < ITERS:
            basis.append(image / length[None, :, None])
    weights = least_squares(columns, beta)
    for current in range(ITERS):
        solution = solution + weights[current][None, :, None] * basis[current]
    return solution


def gradient_terms(adjoint, currents, sensitivity):
    sens_real = sensitivity[:, 0][:, None, :]
    sens_imag = sensitivity[:, 1][:, None, :]
    load_real = sens_real * currents[:, 0] - sens_imag * currents[:, 1]
    load_imag = sens_real * currents[:, 1] + sens_imag * currents[:, 0]
    return -jnp.sum(adjoint[:, 0] * load_real + adjoint[:, 1] * load_imag, axis=(0, 1))


def body(impedance, adjoint_source, currents, sensitivity, owner):
    panel_real = impedance[0, 0]
    panel_imag = impedance[0, 1]
    source = adjoint_source[0]
    width = panel_real.shape[0]
    excite = source.shape[1]

    def row_operator(vector):
        image = apply_adjoint(panel_real, panel_imag, vector)
        return lax.psum_scatter(
            jnp.transpose(image.reshape(2, excite, 1 * lax.axis_size("blk"), width), (2, 0, 1, 3)),
            "blk",
            scatter_dimension=0,
            tiled=True,
        )[0]

    def row_total(local):
        return lax.psum(local, "blk")

    def row_ortho(stacked, image):
        local = jnp.einsum("jckn,ckn->kj", stacked, image, precision=HIGH)
        coeffs = lax.psum(local, "blk")
        image = image - jnp.einsum("jckn,kj->ckn", stacked, coeffs, precision=HIGH)
        length = jnp.sqrt(row_total(jnp.sum(image * image, axis=(0, 2))) + EPS)
        return (image, coeffs, length)

    solution = restarted_solve(source, row_operator, row_total, row_ortho)
    terms = gradient_terms(solution[None], currents, sensitivity)
    design_ids = jnp.arange(DESIGN, dtype=jnp.int32)
    one_hot = (owner[:, None] == design_ids[None, :]).astype(jnp.float32)
    partial_grad = jnp.dot(
        terms[None, :], one_hot, precision=HIGH, preferred_element_type=jnp.float32
    )[0]
    summed_grad = lax.psum(partial_grad, ("band", "blk"))
    share = DESIGN // lax.axis_size(("band", "blk"))
    design = lax.dynamic_slice_in_dim(
        summed_grad, lax.axis_index(("band", "blk")) * share, share, 0
    )
    return (solution[None], design)


def solution(mesh):
    placed = (
        P("band", None, "blk", None),
        P("band", None, None, "blk"),
        P("band", None, None, "blk"),
        P("band", None, "blk"),
        P("blk"),
    )
    return jax.shard_map(
        body,
        mesh=mesh,
        in_specs=placed,
        out_specs=(P("band", None, None, "blk"), P(("band", "blk"))),
        check_vma=False,
    )
```

profile of v0, /device:TPU:1, one launch (start us, length us, event | category | flops | bytes accessed | tf_op | source)
XLA Modules:
  0.0 904.3 jit_solution(11899428549222248003)
XLA Ops:
  8.2 35.3 %psum.84 = f32[32]{0:T(128)S(1)} all-reduce(f32[32]{0:T(128)S(1)} %fusion.51), channel_id=1, replica_groups=mesh['band'=8,'blk'=16] {'blk'}, use_global_device_ids=true, to_apply=%region_1.0 | all-reduce | flops 32 | bytes 256 | tf_op jit(solution)/shard_map/psum | solution.py:96
  44.5 8.2 fusion.18
  52.7 8.2 fusion.8
  64.3 67.5 %reduce-scatter.6.cloned.1.call-done = f32[1,2,32,384]{3,2,1,0:T(8,128)} async-done(((f32[16,2,32,384]{3,2,1,0:T(8,128)}), f32[1,2,32,384]{3,2,1,0:T(8,128)}) %reduce-scatter.6.cloned.1.call-update) | async-done | bytes 98320 | tf_op jit(solution)/shard_map/reduce_scatter | solution.py:88
  132.8 35.0 %psum.85 = f32[32]{0:T(128)S(1)} all-reduce(f32[32]{0:T(128)S(1)} %fusion.50), channel_id=1, replica_groups=mesh['band'=8,'blk'=16] {'blk'}, use_global_device_ids=true, to_apply=%region_3.0 | all-reduce | flops 32 | bytes 256 | tf_op jit(solution)/shard_map/psum | solution.py:100
  168.9 33.6 %psum.86 = f32[32]{0:T(128)S(1)} all-reduce(f32[32]{0:T(128)S(1)} %multiply_reduce_fusion.3), channel_id=1, replica_groups=mesh['band'=8,'blk'=16] {'blk'}, use_global_device_ids=true, to_apply=%region_5.0 | all-reduce | flops 32 | bytes 256 | tf_op jit(solution)/shard_map/psum | solution.py:96
  203.5 8.2 fusion.16
  211.7 8.2 fusion.6
  222.3 64.0 %reduce-scatter.8.cloned.1.call-done = f32[1,2,32,384]{3,2,1,0:T(8,128)} async-done(((f32[16,2,32,384]{3,2,1,0:T(8,128)}), f32[1,2,32,384]{3,2,1,0:T(8,128)}) %reduce-scatter.8.cloned.1.call-update) | async-done | bytes 98320 | tf_op jit(solution)/shard_map/reduce_scatter | solution.py:88
  286.3 2.5 fusion.46
  288.9 35.1 %psum.87 = f32[32,2]{0,1:T(2,128)S(1)} all-reduce(f32[32,2]{0,1:T(2,128)S(1)} %bitcast.472), channel_id=1, replica_groups=mesh['band'=8,'blk'=16] {'blk'}, use_global_device_ids=true, to_apply=%region_7.0 | all-reduce | flops 64 | bytes 512 | tf_op jit(solution)/shard_map/psum | solution.py:100
  325.9 33.5 %psum.88 = f32[32]{0:T(128)S(1)} all-reduce(f32[32]{0:T(128)S(1)} %multiply_reduce_fusion.2), channel_id=1, replica_groups=mesh['band'=8,'blk'=16] {'blk'}, use_global_device_ids=true, to_apply=%region_9.0 | all-reduce | flops 32 | bytes 256 | tf_op jit(solution)/shard_map/psum | solution.py:96
  360.5 8.2 fusion.14
  368.7 8.2 fusion.4
  379.3 63.9 %reduce-scatter.10.cloned.1.call-done = f32[1,2,32,384]{3,2,1,0:T(8,128)} async-done(((f32[16,2,32,384]{3,2,1,0:T(8,128)}), f32[1,2,32,384]{3,2,1,0:T(8,128)}) %reduce-scatter.10.cloned.1.call-update) | async-done | bytes 98320 | tf_op jit(solution)/shard_map/reduce_scatter | solution.py:88
  443.3 2.5 fusion.38
  445.9 35.1 %psum.89 = f32[32,3]{0,1:T(4,128)S(1)} all-reduce(f32[32,3]{0,1:T(4,128)S(1)} %bitcast.470), channel_id=1, replica_groups=mesh['band'=8,'blk'=16] {'blk'}, use_global_device_ids=true, to_apply=%region_11.0 | all-reduce | flops 96 | bytes 768 | tf_op jit(solution)/shard_map/psum | solution.py:100
  483.0 33.8 %psum.90 = f32[32]{0:T(128)S(1)} all-reduce(f32[32]{0:T(128)S(1)} %multiply_reduce_fusion.1), channel_id=1, replica_groups=mesh['band'=8,'blk'=16] {'blk'}, use_global_device_ids=true, to_apply=%region_13.0 | all-reduce | flops 32 | bytes 256 | tf_op jit(solution)/shard_map/psum | solution.py:96
  517.7 8.2 fusion.12
  526.0 8.2 fusion.2
  536.6 64.0 %reduce-scatter.12.cloned.1.call-done = f32[1,2,32,384]{3,2,1,0:T(8,128)} async-done(((f32[16,2,32,384]{3,2,1,0:T(8,128)}), f32[1,2,32,384]{3,2,1,0:T(8,128)}) %reduce-scatter.12.cloned.1.call-update) | async-done | bytes 98320 | tf_op jit(solution)/shard_map/reduce_scatter | solution.py:88
  600.6 2.6 fusion.42
  603.3 35.1 %psum.91 = f32[32,4]{0,1:T(4,128)S(1)} all-reduce(f32[32,4]{0,1:T(4,128)S(1)} %bitcast.471), channel_id=1, replica_groups=mesh['band'=8,'blk'=16] {'blk'}, use_global_device_ids=true, to_apply=%region_15.0 | all-reduce | flops 128 | bytes 1024 | tf_op jit(solution)/shard_map/psum | solution.py:100
  640.4 33.5 %psum.92 = f32[32]{0:T(128)S(1)} all-reduce(f32[32]{0:T(128)S(1)} %multiply_reduce_fusion), channel_id=1, replica_groups=mesh['band'=8,'blk'=16] {'blk'}, use_global_device_ids=true, to_apply=%region_17.0 | all-reduce | flops 32 | bytes 256 | tf_op jit(solution)/shard_map/psum | solution.py:96
  674.9 8.2 fusion.10
  683.2 8.2 fusion
  694.4 63.3 %reduce-scatter.14.cloned.1.call-done = f32[1,2,32,384]{3,2,1,0:T(8,128)} async-done(((f32[16,2,32,384]{3,2,1,0:T(8,128)}), f32[1,2,32,384]{3,2,1,0:T(8,128)}) %reduce-scatter.14.cloned.1.call-update) | async-done | bytes 98320 | tf_op jit(solution)/shard_map/reduce_scatter | solution.py:88
  757.8 2.8 fusion.34
  760.7 35.0 %psum.93 = f32[32,5]{0,1:T(8,128)S(1)} all-reduce(f32[32,5]{0,1:T(8,128)S(1)} %bitcast.468), channel_id=1, replica_groups=mesh['band'=8,'blk'=16] {'blk'}, use_global_device_ids=true, to_apply=%region_19.0 | all-reduce | flops 160 | bytes 1280 | tf_op jit(solution)/shard_map/psum | solution.py:100
  797.0 33.3 %psum.94 = f32[32]{0:T(128)S(1)} all-reduce(f32[32]{0:T(128)S(1)} %fusion.49), channel_id=1, replica_groups=mesh['band'=8,'blk'=16] {'blk'}, use_global_device_ids=true, to_apply=%region_21.0 | all-reduce | flops 32 | bytes 256 | tf_op jit(solution)/shard_map/psum | solution.py:96
  830.7 2.1 fusion.30
  832.8 64.3 %psum.95 = f32[4096]{0:T(1024)S(1)} all-reduce(f32[4096]{0:T(1024)S(1)} %bitcast.469), channel_id=1, replica_groups=mesh['band'=8,'blk'=16] {'band','blk'}, use_global_device_ids=true, to_apply=%region_23.0 | all-reduce | flops 4096 | bytes 32768 | tf_op jit(solution)/shard_map/psum | solution.py:112
  (99 shorter events, 29.7 us)
Async XLA Ops:
  7.2 124.6 %reduce-scatter.6.cloned.1.call-start = ((), (), s32[]{:S(2)}) async-start(), calls=%async_computation.5 | async-start | bytes 1671168 | tf_op jit(solution)/shard_map/reduce_scatter | solution.py:88
  63.3 0.9 copy-start
  63.3 223.0 %reduce-scatter.8.cloned.1.call-start = ((), (), s32[]{:S(2)}) async-start(), calls=%async_computation.6 | async-start | bytes 1671168 | tf_op jit(solution)/shard_map/reduce_scatter | solution.py:88
  222.3 221.0 %reduce-scatter.10.cloned.1.call-start = ((), (), s32[]{:S(2)}) async-start(), calls=%async_computation.7 | async-start | bytes 1671168 | tf_op jit(solution)/shard_map/reduce_scatter | solution.py:88
  379.3 221.3 %reduce-scatter.12.cloned.1.call-start = ((), (), s32[]{:S(2)}) async-start(), calls=%async_computation.8 | async-start | bytes 1671168 | tf_op jit(solution)/shard_map/reduce_scatter | solution.py:88
  536.5 221.2 %reduce-scatter.14.cloned.1.call-start = ((), (), s32[]{:S(2)}) async-start(), calls=%async_computation.9 | async-start | bytes 1671168 | tf_op jit(solution)/shard_map/reduce_scatter | solution.py:88
  693.7 0.7 copy-start.4
  693.7 136.9 %copy-start.3 = (f32[1,2,32,384]{3,2,1,0:T(8,128)S(1)}, f32[1,2,32,384]{3,2,1,0:T(8,128)}, u32[]{:S(2)}) copy-start(f32[1,2,32,384]{3,2,1,0:T(8,128)} %param.7) | copy-start | bytes 294916
  693.7 136.9 %copy-start.5 = (s32[384]{0:T(512)S(1)}, s32[384]{0:T(512)}, u32[]{:S(2)}) copy-start(s32[384]{0:T(512)} %param.9) | copy-start | bytes 4612
  757.7 39.1 %copy-start.1 = (f32[1,2,32,384]{3,2,1,0:T(8,128)S(1)}, f32[1,2,32,384]{3,2,1,0:T(8,128)}, u32[]{:S(2)}) copy-start(f32[1,2,32,384]{3,2,1,0:T(8,128)} %reduce-scatter.14.cloned.1.call-done) | copy-start | bytes 294916
  830.6 67.0 %copy-start.2 = (f32[1,2,32,384]{3,2,1,0:T(8,128)}, f32[1,2,32,384]{3,2,1,0:T(8,128)S(1)}, u32[]{:S(2)}) copy-start(f32[1,2,32,384]{3,2,1,0:T(8,128)S(1)} %add_bitcast_fusion) | copy-start | bytes 294916
Sparse Core Ops, SparseCore 0:
  63.4 68.2 reduce-scatter.5
  222.4 63.8 reduce-scatter.7
  379.4 63.8 reduce-scatter.9
  536.7 63.8 reduce-scatter.11
  693.8 63.8 reduce-scatter.13
where the time goes:
time: 910 us; the launch traced here: 904 us
  blocking collectives  442 us (49%)
  waiting for transfers between devices  323 us (35%)
  matrix products  98.8 us (11%)
  other arithmetic  18.9 us (2%)
  between operations  14.5 us (2%)
    reduce_scatter x5, waiting for transfers between devices, row_operator(): lax.psum_scatter(jnp.transpose(image.reshape(2, excite, 1 * lax.axis_size...  323 us
    psum x6, blocking collectives, row_total(): return lax.psum(local, 'blk')  203 us
    psum x5, blocking collectives, row_ortho(): coeffs = lax.psum(local, 'blk')  175 us
    psum x1, blocking collectives, body(): summed_grad = lax.psum(partial_grad, ('band', 'blk'))  64.3 us
    dot_general x5, matrix products, apply_adjoint(): jnp.dot(stacked, panel_real, precision=HIGH, preferred_element_type=jnp.f...  41.2 us
    dot_general x5, matrix products, apply_adjoint(): jnp.dot(stacked, panel_imag, precision=HIGH, preferred_element_type=jnp.f...  41.2 us
  transfers between devices with their start and end apart: 5, of which 5 were waited for; matrix products, arithmetic and copies ran while one was open for 0% of the time, Pallas kernels for 0%

commit v1 on v0

v1 whole, which is shorter than its diff:
```python
import functools

import jax
import jax.numpy as jnp
from jax import lax
from jax.experimental import pallas as pl
from jax.experimental.pallas import tpu as pltpu
from jax.sharding import PartitionSpec as P

ITERS = 5
DESIGN = 4096
EPS = 1e-12
CHIPS = 8
BLK = 16
LANES = 128
STAGING = 3
LAG = 2
MESH = pl.DeviceIdType.MESH
F32 = jnp.float32
BF16 = jnp.bfloat16


def givens_solve(columns, beta):
    count = len(columns)
    cosines, sines, upper = [], [], []
    rhs = [beta] + [jnp.zeros_like(beta) for _ in range(count)]
    for current in range(count):
        column = list(columns[current])
        for earlier in range(current):
            top = cosines[earlier] * column[earlier] + sines[earlier] * column[earlier + 1]
            column[earlier + 1] = (
                cosines[earlier] * column[earlier + 1] - sines[earlier] * column[earlier]
            )
            column[earlier] = top
        radius = jnp.sqrt(
            column[current] * column[current] + column[current + 1] * column[current + 1]
        )
        cosines.append(column[current] / radius)
        sines.append(column[current + 1] / radius)
        column[current] = radius
        upper.append(column[: current + 1])
        rhs[current + 1] = -sines[current] * rhs[current]
        rhs[current] = cosines[current] * rhs[current]
    weights = [None] * count
    for current in reversed(range(count)):
        total = rhs[current]
        for later in range(current + 1, count):
            total = total - upper[later][current] * weights[later]
        weights[current] = total / upper[current][current]
    return weights


def kernel(
    bands,
    share,
    panel,
    source,
    currents,
    sens,
    owner,
    field,
    design,
    staging,
    high,
    low,
    lhs,
    both,
    summed,
    pair_in,
    ring_in,
    basis,
    images,
    small_out,
    small_in,
    band_out,
    band_in,
    load_sem,
    pair_send,
    pair_recv,
    ring_send,
    ring_recv,
    small_send,
    small_recv,
    band_send,
    band_recv,
):
    excite = source.shape[0] // 2
    rows = 2 * excite
    width = source.shape[1]
    chunks = width // LANES
    wide = 2 * width
    band = lax.axis_index("band")
    blk = lax.axis_index("blk")
    core = blk % 2
    partner = blk + 1 - 2 * core
    along_x = (blk // 2) % 2
    along_z = blk // 4

    def chip_of(step):
        offset = CHIPS - 1 - step
        return ((along_z + offset % 4) % 4) * 2 + (along_x + offset // 4) % 2

    def load(step):
        slot = step % STAGING
        cols = pl.ds(pl.multiple_of(chip_of(step) * wide, wide), wide)
        return pltpu.make_async_copy(panel.at[:, cols], staging.at[slot], load_sem.at[slot])

    for step in range(STAGING):
        load(step).start()

    barrier = pltpu.get_barrier_semaphore()

    def greet_blk(step, carry):
        pl.semaphore_signal(
            barrier, inc=1, device_id={"blk": (blk + step) % BLK}, device_id_type=MESH
        )
        return carry

    def greet_band(step, carry):
        pl.semaphore_signal(
            barrier, inc=1, device_id={"band": (band + step) % bands}, device_id_type=MESH
        )
        return carry

    lax.fori_loop(1, BLK, greet_blk, 0)
    if bands > 1:
        lax.fori_loop(1, bands, greet_band, 0)
    pl.semaphore_wait(barrier, BLK - 1 + bands - 1)

    def pair_copy(step, parity):
        return pltpu.make_async_remote_copy(
            src_ref=both.at[step, 1 - core],
            dst_ref=pair_in.at[parity, step],
            send_sem=pair_send.at[step],
            recv_sem=pair_recv.at[parity, step],
            device_id={"blk": partner},
            device_id_type=MESH,
        )

    def ring_copy(step, parity):
        return pltpu.make_async_remote_copy(
            src_ref=summed.at[step],
            dst_ref=ring_in.at[parity, step],
            send_sem=ring_send.at[step],
            recv_sem=ring_recv.at[parity, step],
            device_id={"blk": chip_of(step) * 2 + core},
            device_id_type=MESH,
        )

    def small_copy(step, parity):
        return pltpu.make_async_remote_copy(
            src_ref=small_out.at[parity],
            dst_ref=small_in.at[parity, step],
            send_sem=small_send.at[step],
            recv_sem=small_recv.at[parity, step],
            device_id={"blk": (blk + step) % BLK},
            device_id_type=MESH,
        )

    def band_copy(step):
        return pltpu.make_async_remote_copy(
            src_ref=band_out,
            dst_ref=band_in.at[step],
            send_sem=band_send.at[step],
            recv_sem=band_recv.at[step],
            device_id={"band": (band + step) % bands},
            device_id_type=MESH,
        )

    def small_start(parity):
        def start(step, carry):
            small_copy(step, parity).start()
            return carry

        lax.fori_loop(1, BLK, start, 0)

    def small_wait(parity):
        def wait(step, carry):
            small_copy(step, parity).wait()
            return carry

        lax.fori_loop(1, BLK, wait, 0)

    def set_lhs(pieces):
        swapped = [jnp.concatenate([p[excite:], -p[:excite]], axis=0) for p in pieces]
        for place, piece in enumerate(list(pieces) + swapped):
            cols = slice(place * LANES, (place + 1) * LANES)
            top = piece.astype(BF16)
            lhs[0:rows, cols] = top
            lhs[rows : 2 * rows, cols] = (piece - top.astype(F32)).astype(BF16)

    def split(step):
        slot = step % STAGING
        load(step).wait()

        def convert(part, carry):
            here = pl.ds(pl.multiple_of(part * 16, 16), 16)
            value = staging[slot, here, :]
            top = value.astype(BF16)
            high[step, here, :] = top
            low[step, here, :] = (value - top.astype(F32)).astype(BF16)
            return carry

        lax.fori_loop(0, 2 * width // 16, convert, 0, unroll=4)

        @pl.when(step + STAGING < CHIPS)
        def _():
            load(step + STAGING).start()

    def multiply(step):
        first = jnp.dot(lhs[...], high[step], preferred_element_type=F32)
        second = jnp.dot(lhs[0:rows, :], low[step], preferred_element_type=F32)
        image = first[:rows] + first[rows:] + second
        for dest in range(2):
            for chunk in range(chunks):
                lane = (dest * chunks + chunk) * LANES
                both[step, dest, chunk * rows : (chunk + 1) * rows, :] = image[
                    :, lane : lane + LANES
                ]

    def forward(step, parity):
        pair_copy(step, parity).wait()
        summed[step] = both[step, core] + pair_in[parity, step]

    def apply(stage):
        parity = stage % 2

        def body(step, carry):
            @pl.when(step < CHIPS)
            def _():
                if stage == 0:
                    split(step)
                multiply(step)
                pair_copy(step, parity).start()

            @pl.when(step >= LAG)
            def _():
                forward(step - LAG, parity)
                ring_copy(step - LAG, parity).start()

            return carry

        lax.fori_loop(0, CHIPS - 1 + LAG, body, 0)

    def collect(stage):
        parity = stage % 2
        forward(CHIPS - 1, parity)

        def wait(step, carry):
            ring_copy(step, parity).wait()
            return carry

        lax.fori_loop(0, CHIPS - 1, wait, 0)
        pieces = []
        for chunk in range(chunks):
            here = slice(chunk * rows, (chunk + 1) * rows)
            total = summed[CHIPS - 1, here, :]
            for step in range(CHIPS - 1):
                total = total + ring_in[parity, step, here, :]
            pieces.append(total)
        return pieces

    def get(store, index):
        return [store[index, c * rows : (c + 1) * rows, :] for c in range(chunks)]

    def put(store, index, pieces):
        for c in range(chunks):
            store[index, c * rows : (c + 1) * rows, :] = pieces[c]

    lane_of = lax.broadcasted_iota(jnp.int32, (excite, LANES), 1)
    groups = LANES // excite

    def inner_local(a, b):
        total = a[0] * b[0]
        for c in range(1, chunks):
            total = total + a[c] * b[c]
        total = total[:excite] + total[excite:]
        return jnp.sum(total, axis=1, keepdims=True)

    def small_send_products(products, parity):
        stacked = [jnp.zeros((excite, LANES), F32) for _ in range(groups)]
        for q, (a, b) in enumerate(products):
            value = inner_local(a, b)
            g, place = q % groups, q // groups
            stacked[g] = jnp.where(lane_of == place, value, stacked[g])
        tile = jnp.transpose(jnp.concatenate(stacked, axis=0))
        small_out[parity] = tile[0:8]
        small_start(parity)

    def small_result(count, parity):
        small_wait(parity)
        total = small_out[parity]
        for step in range(1, BLK):
            total = total + small_in[parity, step]
        turned = jnp.transpose(total)
        found = []
        for q in range(count):
            g, place = q % groups, q // groups
            column = turned[g * excite : (g + 1) * excite, place : place + 1]
            found.append(jnp.broadcast_to(column, (excite, LANES)))
        return found

    def tall(value):
        return jnp.concatenate([value, value], axis=0)

    def combine(lead, scale, coeffs, vectors):
        scale = tall(scale)
        out = [piece * scale for piece in lead]
        for coeff, vector in zip(coeffs, vectors):
            coeff = tall(coeff)
            out = [o - coeff * p for o, p in zip(out, vector)]
        return out

    start = [source[:, c * LANES : (c + 1) * LANES] for c in range(chunks)]
    put(basis, 0, start)
    set_lhs(start)

    norms, inverse, gram, columns = [], [], {}, []
    coeffs = []
    for stage in range(ITERS):
        parity = stage % 2
        apply(stage)
        newest = stage - 1
        if stage == 0:
            products = [(start, start)]
        else:
            if stage > 1:
                fresh = combine(
                    get(images, newest - 1),
                    inverse[newest - 1],
                    coeffs,
                    [get(basis, i) for i in range(newest)],
                )
                put(basis, newest, fresh)
            vectors = [get(basis, i) for i in range(stage)]
            products = [(v, get(images, newest)) for v in vectors]
            if stage > 1:
                products += [(v, vectors[newest]) for v in vectors]
        small_send_products(products, parity)
        found = small_result(len(products), parity)
        if stage == 0:
            gram[0, 0] = found[0]
            norms.append(jnp.sqrt(found[0] + EPS))
            inverse.append(1.0 / norms[0])
        else:
            if stage > 1:
                for i in range(stage):
                    gram[i, newest] = gram[newest, i] = found[stage + i]
                norms.append(jnp.sqrt(gram[newest, newest] + EPS))
                inverse.append(1.0 / norms[newest])
            column = [found[i] * inverse[i] * inverse[newest] for i in range(stage)]
            columns.append(column)
            coeffs = [column[i] * inverse[i] for i in range(stage)]
        pieces = collect(stage)
        if stage == 0:
            put(images, 0, pieces)
        else:
            pieces = combine(
                pieces, inverse[newest], coeffs, [get(images, i) for i in range(stage)]
            )
            put(images, stage, pieces)
        if stage + 1 < ITERS:
            set_lhs(pieces)

    last = ITERS - 1
    fresh = combine(
        get(images, last - 1), inverse[last - 1], coeffs, [get(basis, i) for i in range(last)]
    )
    put(basis, last, fresh)
    vectors = [get(basis, i) for i in range(ITERS)]
    image = get(images, last)
    products = [(v, image) for v in vectors] + [(v, fresh) for v in vectors] + [(image, image)]
    small_send_products(products, ITERS % 2)
    found = small_result(len(products), ITERS % 2)
    for i in range(ITERS):
        gram[i, last] = gram[last, i] = found[ITERS + i]
    norms.append(jnp.sqrt(gram[last, last] + EPS))
    inverse.append(1.0 / norms[last])
    column = [found[i] * inverse[i] * inverse[last] for i in range(ITERS)]
    square = found[2 * ITERS] * inverse[last] * inverse[last]
    scaled = [column[i] * inverse[i] for i in range(ITERS)]
    for i in range(ITERS):
        inside = -2.0 * column[i]
        for j in range(ITERS):
            inside = inside + gram[i, j] * inverse[i] * scaled[j]
        square = square + column[i] * inside
    columns.append(column)
    lengths = norms[1:] + [jnp.sqrt(jnp.maximum(square, 0.0) + EPS)]
    columns = [columns[j] + [lengths[j]] for j in range(ITERS)]
    weights = givens_solve(columns, norms[0])
    solved = None
    for j in range(ITERS):
        scale = tall(weights[j] * inverse[j])
        part = [scale * p for p in vectors[j]]
        solved = part if solved is None else [s + p for s, p in zip(solved, part)]

    terms = []
    for c in range(chunks):
        here = slice(c * LANES, (c + 1) * LANES)
        field[:, here] = solved[c]
        sens_r, sens_i = sens[0:1, here], sens[1:2, here]
        cur_r, cur_i = currents[0:excite, here], currents[excite:rows, here]
        load_r = sens_r * cur_r - sens_i * cur_i
        load_i = sens_r * cur_i + sens_i * cur_r
        value = solved[c][:excite] * load_r + solved[c][excite:] * load_i
        terms.append(-jnp.sum(value, axis=0, keepdims=True))
    pad = jnp.zeros((8 - chunks, LANES), F32)
    band_out[...] = jnp.concatenate(terms + [pad], axis=0)
    total = band_out[...]
    if bands > 1:

        def band_start(step, carry):
            band_copy(step).start()
            return carry

        def band_wait(step, carry):
            band_copy(step).wait()
            return carry

        lax.fori_loop(1, bands, band_start, 0)
        lax.fori_loop(1, bands, band_wait, 0)
        for step in range(1, bands):
            total = total + band_in[step]
    parity = (ITERS + 1) % 2
    small_out[parity] = jnp.concatenate(
        [total[0:chunks], owner[0:chunks, :], jnp.zeros((8 - 2 * chunks, LANES), F32)], axis=0
    )
    small_start(parity)
    small_wait(parity)
    first_design = (band * BLK + blk) * share
    mine = (first_design + lax.broadcasted_iota(jnp.int32, (share, LANES), 0)).astype(F32)
    held = jnp.zeros((share, LANES), F32)
    for step in range(BLK):
        tile = small_out[parity] if step == 0 else small_in[parity, step]
        for c in range(chunks):
            match = tile[chunks + c : chunks + c + 1] == mine
            held = held + jnp.where(match, tile[c : c + 1], 0.0)
    held = jnp.sum(held, axis=1, keepdims=True)
    row_of = lax.broadcasted_iota(jnp.int32, (share, LANES), 0)
    lane = lax.broadcasted_iota(jnp.int32, (share, LANES), 1)
    design[...] = jnp.sum(jnp.where(row_of == lane, held, 0.0), axis=0, keepdims=True)


def body(bands, impedance, adjoint_source, currents, sensitivity, owner):
    width = impedance.shape[2]
    order = impedance.shape[3]
    excite = adjoint_source.shape[2]
    rows = 2 * excite
    tall = width // LANES * rows
    wide = 2 * width
    share = DESIGN // (bands * BLK)
    vmem = pl.BlockSpec(memory_space=pltpu.VMEM)
    dma = pltpu.SemaphoreType.DMA
    chunks = width // LANES
    field, design = pl.pallas_call(
        functools.partial(kernel, bands, share),
        out_shape=(
            jax.ShapeDtypeStruct((rows, width), F32),
            jax.ShapeDtypeStruct((1, LANES), F32),
        ),
        in_specs=[pl.BlockSpec(memory_space=pl.ANY), vmem, vmem, vmem, vmem],
        out_specs=(vmem, vmem),
        scratch_shapes=[
            pltpu.VMEM((STAGING, wide, wide), F32),
            pltpu.VMEM((CHIPS, wide, wide), BF16),
            pltpu.VMEM((CHIPS, wide, wide), BF16),
            pltpu.VMEM((2 * rows, wide), BF16),
            pltpu.VMEM((CHIPS, 2, tall, LANES), F32),
            pltpu.VMEM((CHIPS, tall, LANES), F32),
            pltpu.VMEM((2, CHIPS, tall, LANES), F32),
            pltpu.VMEM((2, CHIPS - 1, tall, LANES), F32),
            pltpu.VMEM((ITERS, tall, LANES), F32),
            pltpu.VMEM((ITERS, tall, LANES), F32),
            pltpu.VMEM((2, 8, LANES), F32),
            pltpu.VMEM((2, BLK, 8, LANES), F32),
            pltpu.VMEM((8, LANES), F32),
            pltpu.VMEM((bands, 8, LANES), F32),
            dma((STAGING,)),
            dma((CHIPS,)),
            dma((2, CHIPS)),
            dma((CHIPS,)),
            dma((2, CHIPS)),
            dma((BLK,)),
            dma((2, BLK)),
            dma((bands,)),
            dma((bands,)),
        ],
        compiler_params=pltpu.CompilerParams(
            collective_id=0, has_side_effects=True, vmem_limit_bytes=60 << 20
        ),
        name="adjoint_solve",
    )(
        impedance.reshape(wide, order),
        adjoint_source.reshape(rows, width),
        currents.reshape(rows, width),
        sensitivity.reshape(2, width),
        owner.astype(F32).reshape(chunks, LANES),
    )
    return field.reshape(1, 2, excite, width), design[0, :share]


def solution(mesh):
    placed = (
        P("band", None, "blk", None),
        P("band", None, None, "blk"),
        P("band", None, None, "blk"),
        P("band", None, "blk"),
        P("blk"),
    )
    return jax.shard_map(
        functools.partial(body, mesh.shape["band"]),
        mesh=mesh,
        in_specs=placed,
        out_specs=(P("band", None, None, "blk"), P(("band", "blk"))),
        check_vma=False,
    )
```

time: 910 us -> 118 us (0.13)
  blocking collectives: 442 us -> 0 us
  waiting for transfers between devices: 323 us -> 0 us
  Pallas kernels: 0 us -> 113 us
  matrix products: 98.8 us -> 0 us
  other arithmetic: 18.9 us -> 1.26 us
  between operations: 14.5 us -> 0.64 us
    psum x12 -> x0, blocking collectives: 442 us -> none  [the longest x6 203 us: row_total(): return lax.psum(local, 'blk')]
    reduce_scatter x5 -> x0, waiting for transfers between devices: 323 us -> none  [row_operator(): lax.psum_scatter(jnp.transpose(image.reshape(2, excite, 1 * lax.axis_size...]
    pallas_call x0 -> x1, Pallas kernels: none -> 113 us  [body(): pl.pallas_call(functools.partial(kernel, bands, share), out_shape=(jax.Sh...]
    dot_general x19 -> x0, matrix products: 98.8 us -> none  [the longest x5 41.2 us: apply_adjoint(): jnp.dot(stacked, panel_real, precision=HIGH, preferred_element_type=jnp.f...]
  transfers between devices with their start and end apart: 5 -> 0, of which waited for: 5 -> 0; matrix products, arithmetic and copies ran while one was open for 0% -> 0% of each run, Pallas kernels for 0% -> 0%
where the time goes in v1:
time: 118 us; the launch traced here: 117 us
  Pallas kernels  113 us (96%)
  local copies, waits for them, and re-layouts  2.73 us (2%)
  other arithmetic  1.26 us (1%)
    pallas_call x1, Pallas kernels, body(): pl.pallas_call(functools.partial(kernel, bands, share), out_shape=(jax.Sh...  113 us

profile of v1, /device:TPU:1, one launch (start us, length us, event | category | flops | bytes accessed | tf_op | source)
XLA Modules:
  0.0 117.3 jit_solution(3969816228319891676)
XLA Ops:
  0.6 1.3 %convert_bitcast_fusion.owner = f32[3,128]{1,0:T(4,128)} fusion(s32[384]{0:T(512)} %param.9), kind=kLoop, calls=%fused_computation | loop fusion | flops 384 | bytes 3072 | tf_op jit(solution)/shard_map/reshape | solution.py:497
  1.9 112.7 %adjoint_solve.1 = (f32[64,384]{1,0:T(8,128)}, f32[1,128]{1,0:T(1,128)}) custom-call(f32[768,6144]{1,0:T(8,128)} %bitcast.9, f32[64,384]{1,0:T(8,128)} %bitcast.10, f32[64,384]{1,0:T(8,128)} %bitcast.11, f32[2,384]{1,0:T(2,128)} %bitcast.13, f32[3,128]{1,0:T(4,128)} %convert_bitcast_fusion.owner), custom_call_target="tpu_custom_call" | custom-call | tf_op jit(solution)/shard_map/adjoint_solve/pallas_call | solution.py:455
  114.6 1.2 %slice_bitcast_fusion = f32[32]{0:T(128)} fusion(f32[1,128]{1,0:T(1,128)} %get-tuple-element.5), kind=kLoop, calls=%fused_computation.1 | loop fusion | bytes 256 | tf_op jit(solution)/shard_map/squeeze | solution.py:499
  115.8 1.5 %copy.8 = f32[1,2,32,384]{3,2,1,0:T(8,128)} copy(f32[1,2,32,384]{3,2,1,0:T(8,128)} %bitcast.12) | data formatting | bytes 196608

commit v2 on v1

v2 whole, which is shorter than its diff:
```python
import functools

import jax
import jax.numpy as jnp
from jax import lax
from jax.experimental import pallas as pl
from jax.experimental.pallas import tpu as pltpu
from jax.sharding import PartitionSpec as P

ITERS = 5
DESIGN = 4096
EPS = 1e-12
CHIPS = 8
BLK = 16
LANES = 128
STAGING = 3
GROUPS = 2
PER_TRIP = 2
TILE = 8
BLOCK_Z = (2, 1, 3, 1, 3, 2, 0, 0)
BLOCK_X = (1, 1, 1, 0, 0, 0, 1, 0)
HOP_Z = (0, 1, 3, 1, 3, 2, 0)
HOP_X = (1, 0, 0, 0, 0, 0, 1)
RELAYED = 3
EARLY = 5
MESH = pl.DeviceIdType.MESH
F32 = jnp.float32
BF16 = jnp.bfloat16


def givens_solve(columns, beta):
    count = len(columns)
    cosines, sines, upper = [], [], []
    rhs = [beta] + [jnp.zeros_like(beta) for _ in range(count)]
    for current in range(count):
        column = list(columns[current])
        for earlier in range(current):
            top = cosines[earlier] * column[earlier] + sines[earlier] * column[earlier + 1]
            column[earlier + 1] = (
                cosines[earlier] * column[earlier + 1] - sines[earlier] * column[earlier]
            )
            column[earlier] = top
        radius = jnp.sqrt(
            column[current] * column[current] + column[current + 1] * column[current + 1]
        )
        cosines.append(column[current] / radius)
        sines.append(column[current + 1] / radius)
        column[current] = radius
        upper.append(column[: current + 1])
        rhs[current + 1] = -sines[current] * rhs[current]
        rhs[current] = cosines[current] * rhs[current]
    weights = [None] * count
    for current in reversed(range(count)):
        total = rhs[current]
        for later in range(current + 1, count):
            total = total - upper[later][current] * weights[later]
        weights[current] = total / upper[current][current]
    return weights


def pick(values, step):
    if isinstance(step, int):
        return values[step]
    total = jnp.int32(0)
    for place, value in enumerate(values):
        if value:
            total = total + jnp.where(step == place, value, 0)
    return total


def kernel(
    bands,
    share,
    panel,
    source_hbm,
    currents_hbm,
    sens_hbm,
    owner_hbm,
    field_hbm,
    design,
    source,
    currents,
    sens,
    owner,
    field,
    staging,
    high,
    low,
    lhs,
    both,
    summed,
    pair_in,
    ring_in,
    basis,
    images,
    small_out,
    small_in,
    band_out,
    band_in,
    load_sem,
    input_sem,
    field_sem,
    pair_send,
    pair_recv,
    ring_send,
    ring_recv,
    small_send,
    small_recv,
    band_send,
    band_recv,
):
    total_excite = source.shape[0] // 2
    excite = total_excite // GROUPS
    rows = 2 * excite
    width = source.shape[1]
    chunks = width // LANES
    data = chunks * rows
    payload = data + 1
    wide = 2 * width
    trips = CHIPS // PER_TRIP
    band = lax.axis_index("band")
    blk = lax.axis_index("blk")
    core = blk % 2
    partner = blk + 1 - 2 * core
    along_x = (blk // 2) % 2
    along_z = blk // 4

    def chip_of(step):
        return ((along_z + pick(BLOCK_Z, step)) % 4) * 2 + (along_x + pick(BLOCK_X, step)) % 2

    def next_chip(step):
        return ((along_z + pick(HOP_Z, step)) % 4) * 2 + (along_x + pick(HOP_X, step)) % 2

    def load(step):
        slot = step % STAGING
        cols = pl.ds(pl.multiple_of(chip_of(step) * wide, wide), wide)
        return pltpu.make_async_copy(panel.at[:, cols], staging.at[slot], load_sem.at[slot])

    pairs = [(source_hbm, source), (currents_hbm, currents), (sens_hbm, sens), (owner_hbm, owner)]
    inputs = [
        pltpu.make_async_copy(src, dst, input_sem.at[i]) for i, (src, dst) in enumerate(pairs)
    ]
    inputs[0].start()
    for step in range(STAGING):
        load(step).start()
    for copy in inputs[1:]:
        copy.start()

    barrier = pltpu.get_barrier_semaphore()

    def greet_blk(step, carry):
        pl.semaphore_signal(
            barrier, inc=1, device_id={"blk": (blk + step) % BLK}, device_id_type=MESH
        )
        return carry

    def greet_band(step, carry):
        pl.semaphore_signal(
            barrier, inc=1, device_id={"band": (band + step) % bands}, device_id_type=MESH
        )
        return carry

    lax.fori_loop(1, BLK, greet_blk, 0)
    if bands > 1:
        lax.fori_loop(1, bands, greet_band, 0)

    def arrived():
        pl.semaphore_wait(barrier, BLK - 1 + bands - 1)

    def pair_copy(group, trip, parity):
        here = pl.ds(trip * PER_TRIP, PER_TRIP)
        return pltpu.make_async_remote_copy(
            src_ref=both.at[group, 1 - core, here, pl.ds(0, payload)],
            dst_ref=pair_in.at[group, parity, here, pl.ds(0, payload)],
            send_sem=pair_send.at[group, trip],
            recv_sem=pair_recv.at[group, parity, trip],
            device_id={"blk": partner},
            device_id_type=MESH,
        )

    def ring_copy(group, step, parity, relayed):
        return pltpu.make_async_remote_copy(
            src_ref=summed.at[group, step, pl.ds(0, payload)],
            dst_ref=ring_in.at[group, parity, step, pl.ds(0, payload)],
            send_sem=ring_send.at[group],
            recv_sem=ring_recv.at[group, parity, relayed],
            device_id={"blk": next_chip(step) * 2 + core},
            device_id_type=MESH,
        )

    def ring_whole(group, parity, first, count, relayed):
        whole = ring_in.at[group, parity, pl.ds(first, count), pl.ds(0, payload)]
        return pltpu.make_async_remote_copy(
            src_ref=whole,
            dst_ref=whole,
            send_sem=ring_send.at[group],
            recv_sem=ring_recv.at[group, parity, relayed],
            device_id={"blk": partner},
            device_id_type=MESH,
        )

    def small_copy(n, use):
        dz, dx, dc = (2, 1, 3, 0)[n // 4], 1 - (n // 2) % 2, 1 - n % 2
        target = ((along_z + dz) % 4) * 4 + ((along_x + dx) % 2) * 2 + (core + dc) % 2
        return pltpu.make_async_remote_copy(
            src_ref=small_out.at[use],
            dst_ref=small_in.at[use, n],
            send_sem=small_send.at[use],
            recv_sem=small_recv.at[use],
            device_id={"blk": target},
            device_id_type=MESH,
        )

    def band_copy(step):
        return pltpu.make_async_remote_copy(
            src_ref=band_out,
            dst_ref=band_in.at[step],
            send_sem=band_send.at[step],
            recv_sem=band_recv.at[step],
            device_id={"band": (band + step) % bands},
            device_id_type=MESH,
        )

    def small_start(use):
        for n in range(BLK - 1):
            small_copy(n, use).start()

    def small_wait(use):
        pltpu.make_async_remote_copy(
            src_ref=small_in.at[use],
            dst_ref=small_in.at[use],
            send_sem=small_send.at[use],
            recv_sem=small_recv.at[use],
            device_id={"blk": partner},
            device_id_type=MESH,
        ).wait()
        total = small_out[use]
        for n in range(BLK - 1):
            total = total + small_in[use, n]
        return total

    def set_lhs(group, pieces):
        swapped = [jnp.concatenate([p[excite:], -p[:excite]], axis=0) for p in pieces]
        for place, piece in enumerate(list(pieces) + swapped):
            cols = slice(place * LANES, (place + 1) * LANES)
            top = piece.astype(BF16)
            lhs[0, group * rows : (group + 1) * rows, cols] = top
            lhs[1, group * rows : (group + 1) * rows, cols] = (piece - top.astype(F32)).astype(
                BF16
            )

    def split(step):
        slot = step % STAGING
        load(step).wait()

        def convert(part, carry):
            here = pl.ds(pl.multiple_of(part * 16, 16), 16)
            value = staging[slot, here, :]
            top = value.astype(BF16)
            high[step, here, :] = top
            low[step, here, :] = (value - top.astype(F32)).astype(BF16)
            return carry

        lax.fori_loop(0, 2 * width // 16, convert, 0, unroll=4)

        @pl.when(step + STAGING < CHIPS)
        def _():
            load(step + STAGING).start()

    def multiply(groups, step):
        span = slice(groups[0] * rows, (groups[-1] + 1) * rows)
        count = len(groups) * rows
        left = jnp.concatenate([lhs[0, span, :], lhs[1, span, :]], axis=0)
        first = jnp.dot(left, high[step], preferred_element_type=F32)
        second = jnp.dot(lhs[0, span, :], low[step], preferred_element_type=F32)
        image = first[:count] + first[count:] + second
        for place, group in enumerate(groups):
            for dest in range(2):
                for chunk in range(chunks):
                    lane = (dest * chunks + chunk) * LANES
                    both[group, dest, step, chunk * rows : (chunk + 1) * rows, :] = image[
                        place * rows : (place + 1) * rows, lane : lane + LANES
                    ]

    def add_pair(group, trip, parity):
        pair_copy(group, trip, parity).wait()
        for part in range(PER_TRIP):
            step = trip * PER_TRIP + part
            summed[group, step] = both[group, core, step] + pair_in[group, parity, step]

    def forward(group, trip, parity):
        add_pair(group, trip, parity)
        for part in range(PER_TRIP):
            step = trip * PER_TRIP + part

            @pl.when(step < RELAYED)
            def _():
                ring_copy(group, step, parity, 1).start()

            @pl.when((step >= RELAYED) & (step < EARLY))
            def _():
                ring_copy(group, step, parity, 0).start()

    def finish(group, parity):
        ring_whole(group, parity, 0, RELAYED, 1).wait_recv()
        across, along = EARLY, EARLY + 1
        summed[group, across] = summed[group, across] + ring_in[group, parity, 0]
        ring_copy(group, across, parity, 0).start()
        summed[group, along] = (
            summed[group, along] + ring_in[group, parity, 1] + ring_in[group, parity, 2]
        )
        ring_copy(group, along, parity, 0).start()

    def flush(group, stage):
        add_pair(group, trips - 1, stage % 2)
        finish(group, stage % 2)

    def apply(groups, stage, pending):
        parity = stage % 2

        def body(trip, carry):
            for part in range(PER_TRIP):
                if stage == 0:
                    split(trip * PER_TRIP + part)
            for part in range(PER_TRIP):
                multiply(groups, trip * PER_TRIP + part)
            for group in groups:
                pair_copy(group, trip, parity).start()

            @pl.when(trip > 0)
            def _():
                for group in groups:
                    forward(group, trip - 1, parity)

            if pending is not None:

                @pl.when(trip == 0)
                def _():
                    flush(*pending)

            return carry

        lax.fori_loop(0, trips, body, 0)

    def collect(group, stage):
        parity = stage % 2
        ring_whole(group, parity, RELAYED, CHIPS - 1 - RELAYED, 0).wait_recv()
        ring_whole(group, parity, 0, CHIPS - 1, 0).wait_send()

        def gather(here):
            total = summed[group, CHIPS - 1, here, :]
            for step in range(RELAYED, CHIPS - 1):
                total = total + ring_in[group, parity, step, here, :]
            return total

        tile = gather(slice(data, data + 1))
        pieces = [gather(slice(c * rows, (c + 1) * rows)) for c in range(chunks)]
        return pieces, tile

    def get(store, group, index):
        return [store[group, index, c * rows : (c + 1) * rows, :] for c in range(chunks)]

    def put(store, group, index, pieces):
        for c in range(chunks):
            store[group, index, c * rows : (c + 1) * rows, :] = pieces[c]

    lane_of = lax.broadcasted_iota(jnp.int32, (excite, LANES), 1)
    row_of = lax.broadcasted_iota(jnp.int32, (excite, LANES), 0)
    segments = LANES // excite

    def inner_local(a, b):
        total = a[0] * b[0]
        for c in range(1, chunks):
            total = total + a[c] * b[c]
        total = total[:excite] + total[excite:]
        return jnp.sum(total, axis=1, keepdims=True)

    def pack(products):
        lines = []
        for first in range(0, len(products), segments):
            line = jnp.zeros((excite, LANES), F32)
            for q, (a, b) in enumerate(products[first : first + segments]):
                line = jnp.where(lane_of == row_of + q * excite, inner_local(a, b), line)
            lines.append(jnp.sum(line, axis=0, keepdims=True))
        lines.append(jnp.zeros((TILE - len(lines), LANES), F32))
        return jnp.concatenate(lines, axis=0)

    def unpack(tile, count):
        found = []
        for q in range(count):
            line = tile[q // segments : q // segments + 1]
            picked = jnp.where(lane_of == row_of + (q % segments) * excite, line, 0.0)
            value = jnp.sum(picked, axis=1, keepdims=True)
            found.append(jnp.broadcast_to(value, (excite, LANES)))
        return found

    def stamp(group, tile):
        for step in range(CHIPS):
            for dest in range(2):
                both[group, dest, step, data : data + TILE, :] = tile

    def tall(value):
        return jnp.concatenate([value, value], axis=0)

    def combine(lead, scale, coeffs, vectors):
        scale = tall(scale)
        out = [piece * scale for piece in lead]
        for coeff, vector in zip(coeffs, vectors):
            coeff = tall(coeff)
            out = [o - coeff * p for o, p in zip(out, vector)]
        return out

    def source_rows(ref, group, here):
        first = group * excite
        return jnp.concatenate(
            [
                ref[first : first + excite, here],
                ref[total_excite + first : total_excite + first + excite, here],
            ],
            axis=0,
        )

    def begin(group):
        start = [
            source_rows(source, group, slice(c * LANES, (c + 1) * LANES)) for c in range(chunks)
        ]
        put(basis, group, 0, start)
        set_lhs(group, start)
        stamp(group, pack([(start, start)]))
        return {"norms": [], "inverse": [], "gram": {}, "columns": []}

    def absorb(group, stage, state):
        pieces, tile = collect(group, stage)
        newest = stage - 1
        norms, inverse, gram = state["norms"], state["inverse"], state["gram"]
        if stage == 0:
            gram[0, 0] = unpack(tile, 1)[0]
            norms.append(jnp.sqrt(gram[0, 0] + EPS))
            inverse.append(1.0 / norms[0])
            put(images, group, 0, pieces)
            return pieces
        found = unpack(tile, stage if stage == 1 else 2 * stage)
        if stage > 1:
            for i in range(stage):
                gram[i, newest] = gram[newest, i] = found[stage + i]
            norms.append(jnp.sqrt(gram[newest, newest] + EPS))
            inverse.append(1.0 / norms[newest])
        column = [found[i] * inverse[i] * inverse[newest] for i in range(stage)]
        state["columns"].append(column)
        coeffs = [column[i] * inverse[i] for i in range(stage)]
        pieces = combine(
            pieces, inverse[newest], coeffs, [get(images, group, i) for i in range(stage)]
        )
        put(images, group, stage, pieces)
        fresh = combine(
            get(images, group, newest),
            inverse[newest],
            coeffs,
            [get(basis, group, i) for i in range(stage)],
        )
        put(basis, group, stage, fresh)
        return pieces

    def advance(group, stage, state):
        pieces = absorb(group, stage - 1, state)
        set_lhs(group, pieces)
        vectors = [get(basis, group, i) for i in range(stage)]
        products = [(v, pieces) for v in vectors]
        if stage > 1:
            products += [(v, vectors[-1]) for v in vectors]
        stamp(group, pack(products))

    inputs[0].wait()
    states = [begin(group) for group in range(GROUPS)]
    arrived()
    apply(tuple(range(GROUPS)), 0, None)
    for group in range(GROUPS):
        flush(group, 0)
    pending = None
    for stage in range(1, ITERS):
        for group in range(GROUPS):
            advance(group, stage, states[group])
            apply((group,), stage, pending)
            pending = (group, stage)
    flush(*pending)

    for copy in inputs[1:]:
        copy.wait()
    last = ITERS - 1
    for group in range(GROUPS):
        image = absorb(group, last, states[group])
        vectors = [get(basis, group, i) for i in range(ITERS)]
        products = [(v, image) for v in vectors] + [(v, vectors[last]) for v in vectors]
        small_out[group] = pack(products + [(image, image)])
        small_start(group)

    terms = [jnp.zeros((1, LANES), F32) for _ in range(chunks)]
    for group in range(GROUPS):
        found = unpack(small_wait(group), 2 * ITERS + 1)
        norms, inverse = states[group]["norms"], states[group]["inverse"]
        gram, columns = states[group]["gram"], states[group]["columns"]
        for i in range(ITERS):
            gram[i, last] = gram[last, i] = found[ITERS + i]
        norms.append(jnp.sqrt(gram[last, last] + EPS))
        inverse.append(1.0 / norms[last])
        column = [found[i] * inverse[i] * inverse[last] for i in range(ITERS)]
        square = found[2 * ITERS] * inverse[last] * inverse[last]
        scaled = [column[i] * inverse[i] for i in range(ITERS)]
        for i in range(ITERS):
            inside = -2.0 * column[i]
            for j in range(ITERS):
                inside = inside + gram[i, j] * inverse[i] * scaled[j]
            square = square + column[i] * inside
        columns.append(column)
        lengths = norms[1:] + [jnp.sqrt(jnp.maximum(square, 0.0) + EPS)]
        columns = [columns[j] + [lengths[j]] for j in range(ITERS)]
        weights = givens_solve(columns, norms[0])
        solved = None
        for j in range(ITERS):
            scale = tall(weights[j] * inverse[j])
            part = [scale * p for p in get(basis, group, j)]
            solved = part if solved is None else [s + p for s, p in zip(solved, part)]
        for c in range(chunks):
            here = slice(c * LANES, (c + 1) * LANES)
            first = group * excite
            field[first : first + excite, here] = solved[c][:excite]
            field[total_excite + first : total_excite + first + excite, here] = solved[c][excite:]
            sens_r, sens_i = sens[0:1, here], sens[1:2, here]
            current = source_rows(currents, group, here)
            load_r = sens_r * current[:excite] - sens_i * current[excite:]
            load_i = sens_r * current[excite:] + sens_i * current[:excite]
            value = solved[c][:excite] * load_r + solved[c][excite:] * load_i
            terms[c] = terms[c] - jnp.sum(value, axis=0, keepdims=True)

    stored = pltpu.make_async_copy(field, field_hbm, field_sem)
    stored.start()
    band_out[...] = jnp.concatenate(terms + [jnp.zeros((TILE - chunks, LANES), F32)], axis=0)
    total = band_out[...]
    if bands > 1:

        for step in range(1, bands):
            band_copy(step).start()
        for step in range(1, bands):
            band_copy(step).wait()
        for step in range(1, bands):
            total = total + band_in[step]
    owners = [
        owner[c * LANES : (c + 1) * LANES].astype(F32).reshape(1, LANES) for c in range(chunks)
    ]
    small_out[GROUPS] = jnp.concatenate(
        [total[0:chunks]] + owners + [jnp.zeros((TILE - 2 * chunks, LANES), F32)], axis=0
    )
    small_start(GROUPS)
    small_wait(GROUPS)
    first_design = (band * BLK + blk) * share
    mine = (first_design + lax.broadcasted_iota(jnp.int32, (share, LANES), 0)).astype(F32)
    held = jnp.zeros((share, LANES), F32)
    for step in range(BLK):
        tile = small_out[GROUPS] if step == 0 else small_in[GROUPS, step - 1]
        for c in range(chunks):
            match = tile[chunks + c : chunks + c + 1] == mine
            held = held + jnp.where(match, tile[c : c + 1], 0.0)
    held = jnp.sum(held, axis=1, keepdims=True)
    place = lax.broadcasted_iota(jnp.int32, (share, LANES), 0)
    lane = lax.broadcasted_iota(jnp.int32, (share, LANES), 1)
    design[...] = jnp.sum(jnp.where(place == lane, held, 0.0), axis=0, keepdims=True)
    stored.wait()


def body(bands, impedance, adjoint_source, currents, sensitivity, owner):
    width = impedance.shape[2]
    order = impedance.shape[3]
    excite = adjoint_source.shape[2]
    rows = 2 * excite
    chunks = width // LANES
    data = chunks * rows // GROUPS
    block = data + TILE
    wide = 2 * width
    share = DESIGN // (bands * BLK)
    vmem = pl.BlockSpec(memory_space=pltpu.VMEM)
    hbm = pl.BlockSpec(memory_space=pl.ANY)
    dma = pltpu.SemaphoreType.DMA
    field, design = pl.pallas_call(
        functools.partial(kernel, bands, share),
        out_shape=(
            jax.ShapeDtypeStruct((rows, width), F32),
            jax.ShapeDtypeStruct((1, LANES), F32),
        ),
        in_specs=[hbm] * 5,
        out_specs=(hbm, vmem),
        scratch_shapes=[
            pltpu.VMEM((rows, width), F32),
            pltpu.VMEM((rows, width), F32),
            pltpu.VMEM((2, width), F32),
            pltpu.VMEM((width,), jnp.int32),
            pltpu.VMEM((rows, width), F32),
            pltpu.VMEM((STAGING, wide, wide), F32),
            pltpu.VMEM((CHIPS, wide, wide), BF16),
            pltpu.VMEM((CHIPS, wide, wide), BF16),
            pltpu.VMEM((2, rows, wide), BF16),
            pltpu.VMEM((GROUPS, 2, CHIPS, block, LANES), F32),
            pltpu.VMEM((GROUPS, CHIPS, block, LANES), F32),
            pltpu.VMEM((GROUPS, 2, CHIPS, block, LANES), F32),
            pltpu.VMEM((GROUPS, 2, CHIPS - 1, block, LANES), F32),
            pltpu.VMEM((GROUPS, ITERS, data, LANES), F32),
            pltpu.VMEM((GROUPS, ITERS, data, LANES), F32),
            pltpu.VMEM((GROUPS + 1, TILE, LANES), F32),
            pltpu.VMEM((GROUPS + 1, BLK - 1, TILE, LANES), F32),
            pltpu.VMEM((TILE, LANES), F32),
            pltpu.VMEM((bands, TILE, LANES), F32),
            dma((STAGING,)),
            dma((4,)),
            dma,
            dma((GROUPS, CHIPS // PER_TRIP)),
            dma((GROUPS, 2, CHIPS // PER_TRIP)),
            dma((GROUPS,)),
            dma((GROUPS, 2, 2)),
            dma((GROUPS + 1,)),
            dma((GROUPS + 1,)),
            dma((bands,)),
            dma((bands,)),
        ],
        compiler_params=pltpu.CompilerParams(
            collective_id=0, has_side_effects=True, vmem_limit_bytes=60 << 20
        ),
        name="adjoint_solve",
    )(
        impedance.reshape(wide, order),
        adjoint_source.reshape(rows, width),
        currents.reshape(rows, width),
        sensitivity.reshape(2, width),
        owner,
    )
    return field.reshape(1, 2, excite, width), design[0, :share]


def solution(mesh):
    placed = (
        P("band", None, "blk", None),
        P("band", None, None, "blk"),
        P("band", None, None, "blk"),
        P("band", None, "blk"),
        P("blk"),
    )
    return jax.shard_map(
        functools.partial(body, mesh.shape["band"]),
        mesh=mesh,
        in_specs=placed,
        out_specs=(P("band", None, None, "blk"), P(("band", "blk"))),
        check_vma=False,
    )
```

time: 118 us -> 91.3 us (0.77)
  Pallas kernels: 113 us -> 87.8 us
  other arithmetic: 1.26 us -> 0 us
    pallas_call x1, Pallas kernels: 113 us -> 87.8 us  [body(): pl.pallas_call(functools.partial(kernel, bands, share), out_shape=(jax.Sh...]
    reshape x1 -> x0, other arithmetic: 1.26 us -> none  [body(): owner.astype(F32).reshape(chunks, LANES)]
where the time goes in v2:
time: 91.3 us; the launch traced here: 91.2 us
  Pallas kernels  87.8 us (96%)
  local copies, waits for them, and re-layouts  2.73 us (3%)
    pallas_call x1, Pallas kernels, body(): pl.pallas_call(functools.partial(kernel, bands, share), out_shape=(jax.Sh...  87.8 us

profile of v2, /device:TPU:1, one launch (start us, length us, event | category | flops | bytes accessed | tf_op | source)
XLA Modules:
  0.0 91.2 jit_solution(11017507274153316324)
XLA Ops:
  0.6 87.8 %adjoint_solve.1 = (f32[64,384]{1,0:T(8,128)}, f32[1,128]{1,0:T(1,128)}) custom-call(f32[768,6144]{1,0:T(8,128)} %bitcast.7, f32[64,384]{1,0:T(8,128)} %bitcast.8, f32[64,384]{1,0:T(8,128)} %bitcast.9, f32[2,384]{1,0:T(2,128)} %bitcast.11, s32[384]{0:T(512)} %owner_hbm.1), custom_call_target="tpu_custom_call" | custom-call | tf_op jit(solution)/shard_map/adjoint_solve/pallas_call | solution.py:583
  88.4 1.2 %slice_bitcast_fusion = f32[32]{0:T(128)} fusion(f32[1,128]{1,0:T(1,128)} %get-tuple-element.5), kind=kLoop, calls=%fused_computation | loop fusion | bytes 256 | tf_op jit(solution)/shard_map/squeeze | solution.py:634
  89.6 1.5 %copy.8 = f32[1,2,32,384]{3,2,1,0:T(8,128)} copy(f32[1,2,32,384]{3,2,1,0:T(8,128)} %bitcast.10) | data formatting | bytes 196608

commit v3 on v2

--- a/solution.py
+++ b/solution.py
@@ -17,12 +17,14 @@
 GROUPS = 2
 PER_TRIP = 2
 TILE = 8
-BLOCK_Z = (2, 1, 3, 1, 3, 2, 0, 0)
-BLOCK_X = (1, 1, 1, 0, 0, 0, 1, 0)
-HOP_Z = (0, 1, 3, 1, 3, 2, 0)
-HOP_X = (1, 0, 0, 0, 0, 0, 1)
+BLOCK_Z = (2, 1, 3, 2, 0, 1, 3, 0)
+BLOCK_X = (1, 1, 1, 0, 1, 0, 0, 0)
+HOP_Z = (0, 1, 3, 2, 0, 1, 3)
+HOP_X = (1, 0, 0, 0, 1, 0, 0)
 RELAYED = 3
-EARLY = 5
+ACROSS = 3
+ALONG = 4
+DIRECT = 5
 MESH = pl.DeviceIdType.MESH
 F32 = jnp.float32
 BF16 = jnp.bfloat16
@@ -124,6 +126,7 @@
     partner = blk + 1 - 2 * core
     along_x = (blk // 2) % 2
     along_z = blk // 4
+    beside = band + 1 - 2 * (band % 2)
 
     def chip_of(step):
         return ((along_z + pick(BLOCK_Z, step)) % 4) * 2 + (along_x + pick(BLOCK_X, step)) % 2
@@ -163,9 +166,14 @@
     lax.fori_loop(1, BLK, greet_blk, 0)
     if bands > 1:
         lax.fori_loop(1, bands, greet_band, 0)
+        for n in range(CHIPS):
+            far = ((along_z + n // 2) % 4) * 4 + ((along_x + 1) % 2) * 2 + (core + n % 2) % 2
+            pl.semaphore_signal(
+                barrier, inc=1, device_id={"band": beside, "blk": far}, device_id_type=MESH
+            )
 
     def arrived():
-        pl.semaphore_wait(barrier, BLK - 1 + bands - 1)
+        pl.semaphore_wait(barrier, BLK - 1 + (bands - 1 + CHIPS if bands > 1 else 0))
 
     def pair_copy(group, trip, parity):
         here = pl.ds(trip * PER_TRIP, PER_TRIP)
@@ -202,12 +210,15 @@
     def small_copy(n, use):
         dz, dx, dc = (2, 1, 3, 0)[n // 4], 1 - (n // 2) % 2, 1 - n % 2
         target = ((along_z + dz) % 4) * 4 + ((along_x + dx) % 2) * 2 + (core + dc) % 2
+        where = {"blk": target}
+        if use == GROUPS and dx == 1 and bands > 1:
+            where = {"band": beside, "blk": target}
         return pltpu.make_async_remote_copy(
             src_ref=small_out.at[use],
             dst_ref=small_in.at[use, n],
             send_sem=small_send.at[use],
             recv_sem=small_recv.at[use],
-            device_id={"blk": target},
+            device_id=where,
             device_id_type=MESH,
         )
 
@@ -297,50 +308,44 @@
             def _():
                 ring_copy(group, step, parity, 1).start()
 
-            @pl.when((step >= RELAYED) & (step < EARLY))
+            @pl.when(step >= DIRECT)
             def _():
                 ring_copy(group, step, parity, 0).start()
 
-    def finish(group, parity):
+    def flush(group, stage):
+        parity = stage % 2
+        add_pair(group, trips - 1, parity)
+        ring_copy(group, CHIPS - 2, parity, 0).start()
         ring_whole(group, parity, 0, RELAYED, 1).wait_recv()
-        across, along = EARLY, EARLY + 1
-        summed[group, across] = summed[group, across] + ring_in[group, parity, 0]
-        ring_copy(group, across, parity, 0).start()
-        summed[group, along] = (
-            summed[group, along] + ring_in[group, parity, 1] + ring_in[group, parity, 2]
-        )
-        ring_copy(group, along, parity, 0).start()
-
-    def flush(group, stage):
-        add_pair(group, trips - 1, stage % 2)
-        finish(group, stage % 2)
+        summed[group, ACROSS] = summed[group, ACROSS] + ring_in[group, parity, 0]
+        ring_copy(group, ACROSS, parity, 0).start()
+        summed[group, ALONG] = (
+            summed[group, ALONG] + ring_in[group, parity, 1] + ring_in[group, parity, 2]
+        )
+        ring_copy(group, ALONG, parity, 0).start()
 
     def apply(groups, stage, pending):
         parity = stage % 2
 
-        def body(trip, carry):
-            for part in range(PER_TRIP):
-                if stage == 0:
+        def each(trip, between):
+            if stage == 0:
+                for part in range(PER_TRIP):
                     split(trip * PER_TRIP + part)
             for part in range(PER_TRIP):
                 multiply(groups, trip * PER_TRIP + part)
             for group in groups:
                 pair_copy(group, trip, parity).start()
-
-            @pl.when(trip > 0)
-            def _():
-                for group in groups:
-                    forward(group, trip - 1, parity)
-
-            if pending is not None:
-
-                @pl.when(trip == 0)
-                def _():
-                    flush(*pending)
-
+            if between is not None:
+                flush(*between)
+
+        def body(trip, carry):
+            each(trip, None)
+            for group in groups:
+                forward(group, trip - 1, parity)
             return carry
 
-        lax.fori_loop(0, trips, body, 0)
+        each(0, pending)
+        lax.fori_loop(1, trips, body, 0)
 
     def collect(group, stage):
         parity = stage % 2
@@ -565,6 +570,11 @@
     lane = lax.broadcasted_iota(jnp.int32, (share, LANES), 1)
     design[...] = jnp.sum(jnp.where(place == lane, held, 0.0), axis=0, keepdims=True)
     stored.wait()
+
+
+def hand_out(share, field, design, field_out, design_out):
+    field_out[...] = field[...]
+    design_out[...] = design[0, 0:share]
 
 
 def body(bands, impedance, adjoint_source, currents, sensitivity, owner):
@@ -631,7 +641,17 @@
         sensitivity.reshape(2, width),
         owner,
     )
-    return field.reshape(1, 2, excite, width), design[0, :share]
+    field, design = pl.pallas_call(
+        functools.partial(hand_out, share),
+        out_shape=(
+            jax.ShapeDtypeStruct((rows, width), F32),
+            jax.ShapeDtypeStruct((share,), F32),
+        ),
+        in_specs=[vmem, vmem],
+        out_specs=(vmem, vmem),
+        name="hand_out",
+    )(field, design)
+    return field.reshape(1, 2, excite, width), design
 
 
 def solution(mesh):

time: 91.3 us -> 88.2 us (0.966)
  local copies, waits for them, and re-layouts: 2.73 us -> 0 us
    pallas_call x1, Pallas kernels: 87.8 us -> 85.8 us  [body(): pl.pallas_call(functools.partial(kernel, bands, share), out_shape=(jax.Sh...]
    pallas_call x0 -> x1, Pallas kernels: none -> 1.55 us  [body(): pl.pallas_call(functools.partial(hand_out, share), out_shape=(jax.ShapeDt...]
    unnamed x1 -> x0, local copies, waits for them, and re-layouts: 1.54 us -> none
    squeeze x1 -> x0, local copies, waits for them, and re-layouts: 1.19 us -> none  [body(): return (field.reshape(1, 2, excite, width), design[0, :share])]
where the time goes in v3:
time: 88.2 us; the launch traced here: 88 us
  Pallas kernels  87.4 us (99%)
    pallas_call x1, Pallas kernels, body(): pl.pallas_call(functools.partial(kernel, bands, share), out_shape=(jax.Sh...  85.8 us

profile of v3, /device:TPU:1, one launch (start us, length us, event | category | flops | bytes accessed | tf_op | source)
XLA Modules:
  0.0 88.0 jit_solution(5835666275890203253)
XLA Ops:
  0.6 85.8 %adjoint_solve.1 = (f32[64,384]{1,0:T(8,128)}, f32[1,128]{1,0:T(1,128)}) custom-call(f32[768,6144]{1,0:T(8,128)} %bitcast.5, f32[64,384]{1,0:T(8,128)} %bitcast.6, f32[64,384]{1,0:T(8,128)} %bitcast.7, f32[2,384]{1,0:T(2,128)} %bitcast.8, s32[384]{0:T(512)} %owner_hbm.1), custom_call_target="tpu_custom_call" | custom-call | tf_op jit(solution)/shard_map/adjoint_solve/pallas_call | solution.py:593
  86.5 1.5 %hand_out.1 = (f32[64,384]{1,0:T(8,128)}, f32[32]{0:T(128)}) custom-call(f32[64,384]{1,0:T(8,128)} %get-tuple-element.6.field, f32[1,128]{1,0:T(1,128)} %get-tuple-element.7.design), custom_call_target="tpu_custom_call" | custom-call | tf_op jit(solution)/shard_map/hand_out/pallas_call | solution.py:644

commit v4 on v3

--- a/solution.py
+++ b/solution.py
@@ -207,6 +207,11 @@
             device_id_type=MESH,
         )
 
+    def lines_of(use):
+        if use == GROUPS:
+            return 2 * chunks
+        return pl.cdiv(2 * ITERS + 1, LANES // excite)
+
     def small_copy(n, use):
         dz, dx, dc = (2, 1, 3, 0)[n // 4], 1 - (n // 2) % 2, 1 - n % 2
         target = ((along_z + dz) % 4) * 4 + ((along_x + dx) % 2) * 2 + (core + dc) % 2
@@ -214,8 +219,8 @@
         if use == GROUPS and dx == 1 and bands > 1:
             where = {"band": beside, "blk": target}
         return pltpu.make_async_remote_copy(
-            src_ref=small_out.at[use],
-            dst_ref=small_in.at[use, n],
+            src_ref=small_out.at[use, pl.ds(0, lines_of(use))],
+            dst_ref=small_in.at[use, n, pl.ds(0, lines_of(use))],
             send_sem=small_send.at[use],
             recv_sem=small_recv.at[use],
             device_id=where,
@@ -224,8 +229,8 @@
 
     def band_copy(step):
         return pltpu.make_async_remote_copy(
-            src_ref=band_out,
-            dst_ref=band_in.at[step],
+            src_ref=band_out.at[pl.ds(0, chunks)],
+            dst_ref=band_in.at[step, pl.ds(0, chunks)],
             send_sem=band_send.at[step],
             recv_sem=band_recv.at[step],
             device_id={"band": (band + step) % bands},
@@ -238,8 +243,8 @@
 
     def small_wait(use):
         pltpu.make_async_remote_copy(
-            src_ref=small_in.at[use],
-            dst_ref=small_in.at[use],
+            src_ref=small_in.at[use, :, pl.ds(0, lines_of(use))],
+            dst_ref=small_in.at[use, :, pl.ds(0, lines_of(use))],
             send_sem=small_send.at[use],
             recv_sem=small_recv.at[use],
             device_id={"blk": partner},
@@ -479,9 +484,8 @@
     states = [begin(group) for group in range(GROUPS)]
     arrived()
     apply(tuple(range(GROUPS)), 0, None)
-    for group in range(GROUPS):
-        flush(group, 0)
-    pending = None
+    flush(0, 0)
+    pending = (1, 0)
     for stage in range(1, ITERS):
         for group in range(GROUPS):
             advance(group, stage, states[group])

time: 88.2 us -> 87.7 us (level)
  no operation moved by 1% of the time
where the time goes in v4:
time: 87.7 us; the launch traced here: 87.5 us
  Pallas kernels  86.9 us (99%)
    pallas_call x1, Pallas kernels, body(): pl.pallas_call(functools.partial(kernel, bands, share), out_shape=(jax.Sh...  85.3 us

profile of v4, /device:TPU:1, one launch (start us, length us, event | category | flops | bytes accessed | tf_op | source)
XLA Modules:
  0.0 87.5 jit_solution(6655845780962168842)
XLA Ops:
  0.6 85.3 %adjoint_solve.1 = (f32[64,384]{1,0:T(8,128)}, f32[1,128]{1,0:T(1,128)}) custom-call(f32[768,6144]{1,0:T(8,128)} %bitcast.5, f32[64,384]{1,0:T(8,128)} %bitcast.6, f32[64,384]{1,0:T(8,128)} %bitcast.7, f32[2,384]{1,0:T(2,128)} %bitcast.8, s32[384]{0:T(512)} %owner_hbm.1), custom_call_target="tpu_custom_call" | custom-call | tf_op jit(solution)/shard_map/adjoint_solve/pallas_call | solution.py:597
  86.0 1.5 %hand_out.1 = (f32[64,384]{1,0:T(8,128)}, f32[32]{0:T(128)}) custom-call(f32[64,384]{1,0:T(8,128)} %get-tuple-element.6.field, f32[1,128]{1,0:T(1,128)} %get-tuple-element.7.design), custom_call_target="tpu_custom_call" | custom-call | tf_op jit(solution)/shard_map/hand_out/pallas_call | solution.py:648
